TPU v7x, 32 devices: a whole 2x2x4 slice. The times are simulated.
32 devices in a mesh: groups: 2 (over y), expert: 4 (over z), seq: 4 (over x, core).
Axes of the slice: x: 2, y: 2, z: 4, core: 2. Of those that a mesh axis runs over, the one named last changes fastest.
Arguments:
- inputs: bfloat16 [4096, 1024], P(('groups', 'expert', 'seq')), parts along dimension 0, may hold values from -6 to 6
- grad_out: bfloat16 [4096, 1024], P(('groups', 'expert', 'seq')), parts along dimension 0, may hold values from -4 to 4
- gates: bfloat16 [4096, 4], P(('groups', 'expert', 'seq')), parts along dimension 0, may hold values from 0.049804688 to 0.59765625
- expert_ids: int32 [4096, 4], P(('groups', 'expert', 'seq')), parts along dimension 0, may hold values from 0 to 3, as said below
- slot_index: int32 [4096, 4], P(('groups', 'expert', 'seq')), parts along dimension 0, may hold values from 0 to 127, as said below
- filter_taps: bfloat16 [256, 1024], replicated, may hold values from -0.375 to 0.375
- w_gate: bfloat16 [4, 1024, 512], P('expert', 'seq'), may hold values from -0.1875 to 0.1875
- w_up: bfloat16 [4, 1024, 512], P('expert', 'seq'), may hold values from -0.1875 to 0.1875
- w_down: bfloat16 [4, 512, 1024], P('expert', 'seq'), may hold values from -0.25 to 0.25
Outputs:
- grad_inputs: bfloat16 [4096, 1024], P(('groups', 'expert', 'seq')), parts along dimension 0
- grad_gates: bfloat16 [4096, 4], P(('groups', 'expert', 'seq')), parts along dimension 0
- grad_filter: float32 [512, 1024], P('groups'), parts along dimension 0
- grad_w_gate: bfloat16 [8, 1024, 512], P(('groups', 'expert'), 'seq'), parts along dimension 0
- grad_w_up: bfloat16 [8, 1024, 512], P(('groups', 'expert'), 'seq'), parts along dimension 0
- grad_w_down: bfloat16 [8, 512, 1024], P(('groups', 'expert'), 'seq'), parts along dimension 0
There are 2 independent parts, one for each index of `groups`. A program takes and returns all parts, laid end to end along the dimension named above; an argument that names none is the same for every part. Nothing has to cross between parts.
Inputs may be any that keep to these rules, and one draw needn't show every extreme that they name: `expert_ids`: each row names 4 different experts, and every expert is named by some row. Among the assignments of the 128 rows of one device that name the same expert, slot_index takes each of the values 0, 1, ... once, in an order of priority that is not row order; assignments with a slot of 128 or more are dropped.
All inputs are finite; a program needn't handle non-finite values.
Results may differ from a plain program's by a relative error of at most 0.009.
Values may be sent and summed in bfloat16 or wider, within the bound.
A program may use at most 64 MiB of HBM per device.

v0:
```python
import jax
import jax.numpy as jnp
from jax import lax
from jax.sharding import PartitionSpec as P


def from_behind(block, axis, distance):
    devices = range(lax.axis_size(axis))
    route = [(i - distance, i) for i in devices if i - distance in devices]
    return lax.ppermute(block, axis, route)


def depthwise(signal, kernel):
    return lax.conv_general_dilated(
        signal[None],
        kernel[:, None, :],
        (1,),
        "VALID",
        dimension_numbers=("NWC", "WIO", "NWC"),
        feature_group_count=signal.shape[1],
        preferred_element_type=jnp.float32,
    )[0]


def contract(left, right, left_dim, right_dim):
    return lax.dot_general(
        left, right, (((left_dim,), (right_dim,)), ((), ())), preferred_element_type=jnp.float32
    )


def expert_pass(token_rows, scaled_rows, gate_mat, up_mat, down_mat):
    pre_gate = jnp.dot(token_rows, gate_mat, preferred_element_type=jnp.float32)
    pre_up = jnp.dot(token_rows, up_mat, preferred_element_type=jnp.float32)
    sigma = jax.nn.sigmoid(pre_gate)
    swish = pre_gate * sigma
    hidden = (swish * pre_up).astype(jnp.bfloat16)
    outputs = jnp.dot(hidden, down_mat, preferred_element_type=jnp.float32).astype(jnp.bfloat16)
    grad_hidden = contract(scaled_rows, down_mat, 1, 1)
    grad_pre_gate = (grad_hidden * pre_up * (sigma * (1.0 + pre_gate * (1.0 - sigma)))).astype(
        jnp.bfloat16
    )
    grad_pre_up = (grad_hidden * swish).astype(jnp.bfloat16)
    part_gate = contract(token_rows, grad_pre_gate, 0, 0)
    part_up = contract(token_rows, grad_pre_up, 0, 0)
    part_down = contract(hidden, scaled_rows, 0, 0)
    grad_rows = (
        contract(grad_pre_gate, gate_mat, 1, 1) + contract(grad_pre_up, up_mat, 1, 1)
    ).astype(jnp.bfloat16)
    return (grad_rows, outputs, (part_gate, part_up, part_down))


def body(inputs, grad_out, gates, expert_ids, slot_index, filter_taps, w_gate, w_up, w_down):
    tok_count, width = inputs.shape
    taps = filter_taps.shape[0]
    top_count = expert_ids.shape[1]
    experts = lax.axis_size("expert")
    capacity = tok_count * top_count // experts
    reach = taps - 1
    shift_count = (reach + tok_count - 1) // tok_count
    earlier = [from_behind(inputs, "seq", shift_by) for shift_by in range(shift_count, 0, -1)]
    extended = jnp.concatenate(earlier + [inputs], axis=0)[-(tok_count + reach) :]
    filtered = depthwise(extended, filter_taps[::-1]).astype(jnp.bfloat16)
    kept = slot_index < capacity
    dest = jnp.where(kept, expert_ids * capacity + slot_index, experts * capacity).reshape(-1)

    def place(values):
        rest = values.shape[1:]
        empty = jnp.zeros((experts * capacity,) + rest, values.dtype)
        return empty.at[dest].set(values, mode="drop").reshape((experts, capacity) + rest)

    def fetch(buffer):
        rest = buffer.shape[2:]
        flat = buffer.reshape((experts * capacity,) + rest)
        return jnp.take(flat, dest, axis=0, mode="fill", fill_value=0).reshape(
            (tok_count, top_count) + rest
        )

    token_send = place(
        jnp.broadcast_to(filtered[:, None, :], (tok_count, top_count, width)).reshape(-1, width)
    )
    gate_full, up_full, down_full = (
        lax.all_gather(w_gate, "seq", axis=1, tiled=True),
        lax.all_gather(w_up, "seq", axis=1, tiled=True),
        lax.all_gather(w_down, "seq", axis=1, tiled=True),
    )
    gate_mat = gate_full[0]
    up_mat = up_full[0]
    down_mat = down_full[0]
    scaled = (
        gates.astype(jnp.float32)[:, :, None] * grad_out.astype(jnp.float32)[:, None, :]
    ).astype(jnp.bfloat16)
    token_recv, scaled_recv = (
        lax.all_to_all(token_send, "expert", split_axis=0, concat_axis=0, tiled=True),
        lax.all_to_all(
            place(scaled.reshape(-1, width)), "expert", split_axis=0, concat_axis=0, tiled=True
        ),
    )
    grad_rows, outputs, partials = expert_pass(
        token_recv.reshape(-1, width), scaled_recv.reshape(-1, width), gate_mat, up_mat, down_mat
    )
    grad_back, output_back = (
        lax.all_to_all(
            grad_rows.reshape(experts, capacity, width),
            "expert",
            split_axis=0,
            concat_axis=0,
            tiled=True,
        ),
        lax.all_to_all(
            outputs.reshape(experts, capacity, width),
            "expert",
            split_axis=0,
            concat_axis=0,
            tiled=True,
        ),
    )
    output_rows = fetch(output_back)
    grad_gates = jnp.sum(
        grad_out.astype(jnp.float32)[:, None, :] * output_rows.astype(jnp.float32), axis=2
    ).astype(jnp.bfloat16)
    summed_gate, summed_up, summed_down = (
        lax.psum_scatter(
            partials[0][None].astype(jnp.bfloat16), "seq", scatter_dimension=1, tiled=True
        ).astype(jnp.float32),
        lax.psum_scatter(
            partials[1][None].astype(jnp.bfloat16), "seq", scatter_dimension=1, tiled=True
        ).astype(jnp.float32),
        lax.psum_scatter(
            partials[2][None].astype(jnp.bfloat16), "seq", scatter_dimension=1, tiled=True
        ).astype(jnp.float32),
    )
    grad_filtered = jnp.sum(fetch(grad_back).astype(jnp.float32), axis=1).astype(jnp.bfloat16)
    later = [from_behind(grad_filtered, "seq", -shift_by) for shift_by in range(1, shift_count + 1)]
    grad_extended = jnp.concatenate([grad_filtered] + later, axis=0)[: tok_count + reach]
    grad_inputs = depthwise(grad_extended, filter_taps).astype(jnp.bfloat16)
    local_taps = depthwise(extended, grad_filtered)[::-1]
    grad_filter = lax.psum(local_taps, ("expert", "seq"))
    return (
        grad_inputs,
        grad_gates,
        grad_filter,
        summed_gate.astype(jnp.bfloat16),
        summed_up.astype(jnp.bfloat16),
        summed_down.astype(jnp.bfloat16),
    )


def solution(mesh):
    return jax.shard_map(
        body,
        mesh=mesh,
        in_specs=(
            P(("groups", "expert", "seq"), None),
            P(("groups", "expert", "seq"), None),
            P(("groups", "expert", "seq"), None),
            P(("groups", "expert", "seq"), None),
            P(("groups", "expert", "seq"), None),
            P(),
            P("expert", "seq", None),
            P("expert", "seq", None),
            P("expert", "seq", None),
        ),
        out_specs=(
            P(("groups", "expert", "seq"), None),
            P(("groups", "expert", "seq"), None),
            P("groups", None),
            P(("groups", "expert"), "seq", None),
            P(("groups", "expert"), "seq", None),
            P(("groups", "expert"), "seq", None),
        ),
        check_vma=False,
    )
```

profile of v0, /device:TPU:0, one launch (start us, length us, event | category | flops | bytes accessed | tf_op | source)
XLA Modules:
  0.0 352.4 jit_solution(16538734937356647307)
XLA Ops:
  7.9 5.6 %collective-permute-start = (bf16[128,1024]{1,0:T(8,128)(2,1)}, bf16[128,1024]{1,0:T(8,128)(2,1)}, u32[]{:S(2)}, u32[]{:S(2)}) collective-permute-start(bf16[128,1024]{1,0:T(8,128)(2,1)} %param.11), channel_id=1, source_target_pairs={{0,2},{1,3},{4,6},{5,7},{8,10},{9,11},{12,14},{13,15},{16,18},{17,... | collective-permute-start | bytes 786440 | tf_op jit(solution)/shard_map/ppermute | solution.py:10
  22.3 3.6 %scatter_custom_fusion = bf16[512,1024]{1,0:T(8,128)(2,1)} fusion(s32[512]{0:T(512)S(1)} %bitcast.76, f32[512,1024]{1,0:T(8,128)S(1)} %mul.56, f32[512]{0:T(512)S(1)} %reshape.113, bf16[]{:T(256)} %constant.7.clone.1), kind=kCustom, calls=%fused_computation.21 | custom fusion | flops 1048576 | bytes 3147778 | tf_op jit(solution)/shard_map/scatter | solution.py:69
  25.9 5.0 %all-to-all-start = ((bf16[4,128,1024]{2,1,0:T(8,128)(2,1)}), bf16[4,128,1024]{2,1,0:T(8,128)(2,1)}, u32[]{:S(2)}, u32[]{:S(2)}) async-start(bf16[4,128,1024]{2,1,0:T(8,128)(2,1)} %bitcast.1), calls=%async_computation | async-start | bytes 2097152 | tf_op jit(solution)/shard_map/all_to_all | solution.py:94
  33.6 14.0 %convolution_convert_fusion.4 = bf16[1,128,1024]{2,0,1:T(2,128)(2,1)S(1)} fusion(bf16[1,383,1024]{2,1,0:T(8,128)(2,1)S(1)} %fusion.27, bf16[256,1,1024]{2,0,1:T(8,128)(2,1)S(1)} %bitcast.74), kind=kOutput, calls=%fused_computation.17 | convolution fusion | flops 67239936 | bytes 1570816 | tf_op jit(solution)/shard_map/conv_general_dilated | solution.py:14
  49.1 4.2 %scatter_custom_fusion.1 = bf16[512,1024]{1,0:T(8,128)(2,1)} fusion(s32[512]{0:T(512)S(1)} %bitcast.77, bf16[512,1024]{1,0:T(8,128)(2,1)} %reshape.142, bf16[]{:T(256)} %constant.7.clone.1), kind=kCustom, calls=%fused_computation.49 | custom fusion | bytes 1049088 | tf_op jit(solution)/shard_map/scatter | solution.py:69
  56.3 3.5 all-to-all-start.1
  60.6 3.3 fusion.20
  63.8 21.2 %all-to-all-done.1 = bf16[4,128,1024]{2,1,0:T(8,128)(2,1)S(1)} async-done(((bf16[4,128,1024]{2,1,0:T(8,128)(2,1)}), bf16[4,128,1024]{2,1,0:T(8,128)(2,1)S(1)}, u32[]{:S(2)}, u32[]{:S(2)}) %all-to-all-start.1) | async-done | bytes 1048608 | tf_op jit(solution)/shard_map/all_to_all | solution.py:93
  86.0 2.9 fusion.14
  88.9 4.1 %multiply_convert_fusion.2 = (bf16[512,512]{1,0:T(8,128)(2,1)}, bf16[512,512]{1,0:T(8,128)(2,1)S(1)}, bf16[512,512]{1,0:T(8,128)(2,1)S(1)}) fusion(f32[512,512]{1,0:T(8,128)} %fusion.14, f32[512,512]{1,0:T(8,128)} %fusion.20, bf16[512,1024]{1,0:T(8,128)(2,1)} %bitcast.68, bf16[1,1024,512]{2,1,0:T(8,128)(2,1)} %all-gather.6.cloned.1.call-done), kind=kOutput, calls=%fused_computation.35 | convolution fusion | flops 540803072 | bytes 5767168 | tf_op jit(solution)/shard_map/dot_general | solution.py:33
  96.3 3.5 all-to-all-start.2
  100.0 25.0 %all-to-all-done.2 = bf16[4,128,1024]{2,1,0:T(8,128)(2,1)S(1)} async-done(((bf16[4,128,1024]{2,1,0:T(8,128)(2,1)}), bf16[4,128,1024]{2,1,0:T(8,128)(2,1)S(1)}, u32[]{:S(2)}, u32[]{:S(2)}) %all-to-all-start.2) | async-done | bytes 1048608 | tf_op jit(solution)/shard_map/all_to_all | solution.py:102
  132.9 15.1 %fusion.8 = f32[1,256,1024]{2,0,1:T(1,128)S(1)} fusion(bf16[1,383,1024]{2,1,0:T(8,128)(2,1)} %copy-done.4, bf16[128,1,1024]{2,0,1:T(8,128)(2,1)S(1)} %bitcast.72), kind=kOutput, calls=%fused_computation.18 | convolution fusion | flops 67108864 | bytes 2095104 | tf_op jit(solution)/shard_map/conv_general_dilated | solution.py:14
  148.2 5.3 %rev.7 = f32[256,1024]{1,0:T(8,128)} reverse(f32[256,1024]{1,0:T(8,128)S(1)} %bitcast.64), dimensions={0} | reverse | bytes 2097152 | tf_op jit(solution)/shard_map/rev | solution.py:136
  153.6 3.2 fusion.4
  159.7 3.1 convolution_convert_fusion.3
  162.8 3.5 all-to-all-start.3
  169.2 3.1 fusion.2
  172.3 22.6 %all-to-all-done.3 = bf16[4,128,1024]{2,1,0:T(8,128)(2,1)S(1)} async-done(((bf16[4,128,1024]{2,1,0:T(8,128)(2,1)}), bf16[4,128,1024]{2,1,0:T(8,128)(2,1)S(1)}, u32[]{:S(2)}, u32[]{:S(2)}) %all-to-all-start.3) | async-done | bytes 1048608 | tf_op jit(solution)/shard_map/all_to_all | solution.py:109
  201.2 14.0 %fusion.5 = bf16[1,128,1024]{2,0,1:T(2,128)(2,1)S(1)} fusion(bf16[1,383,1024]{2,1,0:T(8,128)(2,1)S(1)} %fusion.26, bf16[256,1,1024]{2,0,1:T(8,128)(2,1)S(1)} %bitcast.73), kind=kOutput, calls=%fused_computation.16 | convolution fusion | flops 67239936 | bytes 1570816 | tf_op jit(solution)/shard_map/conv_general_dilated | solution.py:14
  216.0 44.2 %all-reduce.2.cloned.1.call-done = f32[256,1024]{1,0:T(8,128)} async-done(((f32[256,1024]{1,0:T(8,128)}), f32[256,1024]{1,0:T(8,128)}) %all-reduce.2.cloned.1.call-update) | async-done | bytes 1048592 | tf_op jit(solution)/shard_map/psum | solution.py:137
  260.1 27.1 %reduce-scatter.8.cloned.1.call-done = bf16[1,128,1024]{2,1,0:T(8,128)(2,1)} async-done(((bf16[1,512,1024]{2,1,0:T(8,128)(2,1)}), bf16[1,128,1024]{2,1,0:T(8,128)(2,1)}) %reduce-scatter.8.cloned.1.call-update) | async-done | bytes 262160 | tf_op jit(solution)/shard_map/reduce_scatter | solution.py:128
  287.2 28.0 %reduce-scatter.6.cloned.1.call-done = bf16[1,256,512]{2,1,0:T(8,128)(2,1)} async-done(((bf16[1,1024,512]{2,1,0:T(8,128)(2,1)}), bf16[1,256,512]{2,1,0:T(8,128)(2,1)}) %reduce-scatter.6.cloned.1.call-update) | async-done | bytes 262160 | tf_op jit(solution)/shard_map/reduce_scatter | solution.py:125
  315.3 28.0 %reduce-scatter.4.cloned.1.call-done = bf16[1,256,512]{2,1,0:T(8,128)(2,1)} async-done(((bf16[1,1024,512]{2,1,0:T(8,128)(2,1)}), bf16[1,256,512]{2,1,0:T(8,128)(2,1)}) %reduce-scatter.4.cloned.1.call-update) | async-done | bytes 262160 | tf_op jit(solution)/shard_map/reduce_scatter | solution.py:122
  (77 shorter events, 45.1 us)
Async XLA Ops:
  7.2 53.4 %all-gather.4.cloned.1.call-start = ((), (), s32[]{:S(2)}) async-start(), calls=%async_computation.7 | async-start | bytes 1310720 | tf_op jit(solution)/shard_map/all_gather | solution.py:84
  7.9 24.5 %collective-permute-start = (bf16[128,1024]{1,0:T(8,128)(2,1)}, bf16[128,1024]{1,0:T(8,128)(2,1)}, u32[]{:S(2)}, u32[]{:S(2)}) collective-permute-start(bf16[128,1024]{1,0:T(8,128)(2,1)} %param.11), channel_id=1, source_target_pairs={{0,2},{1,3},{4,6},{5,7},{8,10},{9,11},{12,14},{13,15},{16,18},{17,... | collective-permute-start | bytes 786440 | tf_op jit(solution)/shard_map/ppermute | solution.py:10
  13.5 18.9 %collective-permute-start.1 = (bf16[128,1024]{1,0:T(8,128)(2,1)}, bf16[128,1024]{1,0:T(8,128)(2,1)}, u32[]{:S(2)}, u32[]{:S(2)}) collective-permute-start(bf16[128,1024]{1,0:T(8,128)(2,1)} %param.11), channel_id=1, source_target_pairs={{0,1},{1,2},{2,3},{4,5},{5,6},{6,7},{8,9},{9,10},{10,11},{12,13},{... | collective-permute-start | bytes 786440 | tf_op jit(solution)/shard_map/ppermute | solution.py:10
  22.3 9.4 %copy-start.7 = (bf16[256,1024]{1,0:T(8,128)(2,1)S(1)}, bf16[256,1024]{1,0:T(8,128)(2,1)}, u32[]{:S(2)}) copy-start(bf16[256,1024]{1,0:T(8,128)(2,1)} %param.16) | copy-start | bytes 1572868
  25.9 6.5 %copy-start.9 = (bf16[128,1024]{1,0:T(8,128)(2,1)S(1)}, bf16[128,1024]{1,0:T(8,128)(2,1)}, u32[]{:S(2)}) copy-start(bf16[128,1024]{1,0:T(8,128)(2,1)} %param.11) | copy-start | bytes 786436
  25.9 30.3 %all-to-all-start = ((bf16[4,128,1024]{2,1,0:T(8,128)(2,1)}), bf16[4,128,1024]{2,1,0:T(8,128)(2,1)}, u32[]{:S(2)}, u32[]{:S(2)}) async-start(bf16[4,128,1024]{2,1,0:T(8,128)(2,1)} %bitcast.1), calls=%async_computation | async-start | bytes 2097152 | tf_op jit(solution)/shard_map/all_to_all | solution.py:94
  30.9 32.9 %all-gather.8.cloned.1.call-start = ((), (), s32[]{:S(2)}) async-start(), calls=%async_computation.9 | async-start | bytes 1310720 | tf_op jit(solution)/shard_map/all_gather | solution.py:82
  33.6 14.0 %copy-start.4 = (bf16[1,383,1024]{2,1,0:T(8,128)(2,1)}, bf16[1,383,1024]{2,1,0:T(8,128)(2,1)S(1)}, u32[]{:S(2)}) copy-start(bf16[1,383,1024]{2,1,0:T(8,128)(2,1)S(1)} %fusion.27) | copy-start | bytes 2353156
  56.3 28.7 %all-to-all-start.1 = ((bf16[4,128,1024]{2,1,0:T(8,128)(2,1)}), bf16[4,128,1024]{2,1,0:T(8,128)(2,1)S(1)}, u32[]{:S(2)}, u32[]{:S(2)}) async-start(bf16[4,128,1024]{2,1,0:T(8,128)(2,1)} %bitcast.6), calls=%async_computation.1 | async-start | bytes 2097152 | tf_op jit(solution)/shard_map/all_to_all | solution.py:93
  59.8 29.1 %all-gather.6.cloned.1.call-start = ((), (), s32[]{:S(2)}) async-start(), calls=%async_computation.8 | async-start | bytes 1310720 | tf_op jit(solution)/shard_map/all_gather | solution.py:83
  85.0 1.0 copy-start.1
  88.9 4.1 %copy-start = (bf16[1,1024,512]{2,1,0:T(8,128)(2,1)S(1)}, bf16[1,1024,512]{2,1,0:T(8,128)(2,1)}, u32[]{:S(2)}) copy-start(bf16[1,1024,512]{2,1,0:T(8,128)(2,1)} %all-gather.8.cloned.1.call-done) | copy-start | bytes 3145732
  93.0 3.3 copy-start.6
  93.0 1.6 copy-start.3
  96.3 28.7 %all-to-all-start.2 = ((bf16[4,128,1024]{2,1,0:T(8,128)(2,1)}), bf16[4,128,1024]{2,1,0:T(8,128)(2,1)S(1)}, u32[]{:S(2)}, u32[]{:S(2)}) async-start(bf16[4,128,1024]{2,1,0:T(8,128)(2,1)} %bitcast.65), calls=%async_computation.2 | async-start | bytes 2097152 | tf_op jit(solution)/shard_map/all_to_all | solution.py:102
  99.8 160.3 %all-reduce.2.cloned.1.call-start = ((), (), s32[]{:S(2)}) async-start(), calls=%async_computation.10 | async-start | bytes 2097152 | tf_op jit(solution)/shard_map/psum | solution.py:137
  153.5 3.3 copy-start.2
  153.5 133.7 %reduce-scatter.8.cloned.1.call-start = ((), (), s32[]{:S(2)}) async-start(), calls=%async_computation.13 | async-start | bytes 1310720 | tf_op jit(solution)/shard_map/reduce_scatter | solution.py:128
  156.8 158.5 %reduce-scatter.6.cloned.1.call-start = ((), (), s32[]{:S(2)}) async-start(), calls=%async_computation.12 | async-start | bytes 1310720 | tf_op jit(solution)/shard_map/reduce_scatter | solution.py:125
  162.8 32.1 %all-to-all-start.3 = ((bf16[4,128,1024]{2,1,0:T(8,128)(2,1)}), bf16[4,128,1024]{2,1,0:T(8,128)(2,1)S(1)}, u32[]{:S(2)}, u32[]{:S(2)}) async-start(bf16[4,128,1024]{2,1,0:T(8,128)(2,1)} %bitcast.71), calls=%async_computation.3 | async-start | bytes 2097152 | tf_op jit(solution)/shard_map/all_to_all | solution.py:109
  166.3 177.0 %reduce-scatter.4.cloned.1.call-start = ((), (), s32[]{:S(2)}) async-start(), calls=%async_computation.11 | async-start | bytes 1310720 | tf_op jit(solution)/shard_map/reduce_scatter | solution.py:122
  166.3 33.8 %collective-permute-start.3 = (bf16[128,1024]{1,0:T(8,128)(2,1)S(1)}, bf16[128,1024]{1,0:T(8,128)(2,1)}, u32[]{:S(2)}, u32[]{:S(2)}) collective-permute-start(bf16[128,1024]{1,0:T(8,128)(2,1)S(1)} %reduce_sum.21), channel_id=1, source_target_pairs={{2,0},{3,1},{6,4},{7,5},{10,8},{11,9},{14,12},{15,13},{18,16},{19,... | collective-permute-start | bytes 786440 | tf_op jit(solution)/shard_map/ppermute | solution.py:10
  167.6 32.5 %collective-permute-start.2 = (bf16[128,1024]{1,0:T(8,128)(2,1)S(1)}, bf16[128,1024]{1,0:T(8,128)(2,1)}, u32[]{:S(2)}, u32[]{:S(2)}) collective-permute-start(bf16[128,1024]{1,0:T(8,128)(2,1)S(1)} %reduce_sum.21), channel_id=1, source_target_pairs={{1,0},{2,1},{3,2},{5,4},{6,5},{7,6},{9,8},{10,9},{11,10},{13,12},{... | collective-permute-start | bytes 786440 | tf_op jit(solution)/shard_map/ppermute | solution.py:10
  197.6 3.6 %copy-start.8 = (bf16[256,1024]{1,0:T(8,128)(2,1)S(1)}, bf16[256,1024]{1,0:T(8,128)(2,1)}, u32[]{:S(2)}) copy-start(bf16[256,1024]{1,0:T(8,128)(2,1)} %param.16) | copy-start | bytes 1572868
  (1 other events, 0.8 us)
Sparse Core Ops, SparseCore 0:
  9.6 19.4 all-gather.3
  33.3 17.2 all-gather.7
  62.2 17.1 all-gather.5
  153.6 106.4 all-reduce.1
  263.1 24.1 reduce-scatter.7
  290.3 24.8 reduce-scatter.5
  318.4 24.8 reduce-scatter.3
where the time goes:
time: 353 us; the launch traced here: 352 us
  waiting for transfers between devices  201 us (57%)
  matrix products  67.9 us (19%)
  local copies, waits for them, and re-layouts  30.4 us (9%)
  starting transfers between devices  26.5 us (8%)
  between operations  14.4 us (4%)
  other arithmetic  12.2 us (3%)
    psum x1, waiting for transfers between devices, body(): grad_filter = lax.psum(local_taps, ('expert', 'seq'))  44.2 us
    conv_general_dilated x3, matrix products, depthwise(): lax.conv_general_dilated(signal[None], kernel[:, None, :], (1,), 'VALID',...  43 us
    reduce_scatter x1, waiting for transfers between devices, body(): lax.psum_scatter(partials[1][None].astype(jnp.bfloat16), 'seq', scatter_d...  28 us
    reduce_scatter x1, waiting for transfers between devices, body(): lax.psum_scatter(partials[0][None].astype(jnp.bfloat16), 'seq', scatter_d...  28 us
    reduce_scatter x1, waiting for transfers between devices, body(): lax.psum_scatter(partials[2][None].astype(jnp.bfloat16), 'seq', scatter_d...  27.1 us
    all_to_all x1, waiting for transfers between devices, body(): lax.all_to_all(grad_rows.reshape(experts, capacity, width), 'expert', spl...  25 us
    all_to_all x1, waiting for transfers between devices, body(): lax.all_to_all(outputs.reshape(experts, capacity, width), 'expert', split...  22.6 us
    all_to_all x1, waiting for transfers between devices, body(): lax.all_to_all(token_send, 'expert', split_axis=0, concat_axis=0, tiled=T...  21.2 us
  transfers between devices with their start and end apart: 15, of which 8 were waited for; matrix products, arithmetic and copies ran while one was open for 20% of the time, Pallas kernels for 0%

commit v1 on v0

--- a/solution.py
+++ b/solution.py
@@ -134,7 +134,7 @@
     grad_extended = jnp.concatenate([grad_filtered] + later, axis=0)[: tok_count + reach]
     grad_inputs = depthwise(grad_extended, filter_taps).astype(jnp.bfloat16)
     local_taps = depthwise(extended, grad_filtered)[::-1]
-    grad_filter = lax.psum(local_taps, ("expert", "seq"))
+    grad_filter = lax.psum(lax.psum(local_taps, "seq"), "expert")
     return (
         grad_inputs,
         grad_gates,

time: 353 us -> 339 us (0.960)
  waiting for transfers between devices: 201 us -> 187 us
    reduce_scatter x1, waiting for transfers between devices: 27.1 us -> 3.15 us  [body(): lax.psum_scatter(partials[2][None].astype(jnp.bfloat16), 'seq', scatter_d...]
    psum x1 -> x2, waiting for transfers between devices: 44.2 us -> 54.3 us  [body(): grad_filter = lax.psum(lax.psum(local_taps, 'seq'), 'expert')]
  transfers between devices with their start and end apart: 15 -> 16, of which waited for: 8 -> 8; matrix products, arithmetic and copies ran while one was open for 20% -> 21% of each run, Pallas kernels for 0% -> 0%
where the time goes in v1:
time: 339 us; the launch traced here: 338 us
  waiting for transfers between devices  187 us (55%)
  matrix products  67.6 us (20%)
  local copies, waits for them, and re-layouts  30.4 us (9%)
  starting transfers between devices  26.5 us (8%)
  between operations  14.4 us (4%)
  other arithmetic  12.2 us (4%)
    psum x2, waiting for transfers between devices, body(): grad_filter = lax.psum(lax.psum(local_taps, 'seq'), 'expert')  54.3 us
    conv_general_dilated x3, matrix products, depthwise(): lax.conv_general_dilated(signal[None], kernel[:, None, :], (1,), 'VALID',...  43 us
    reduce_scatter x1, waiting for transfers between devices, body(): lax.psum_scatter(partials[0][None].astype(jnp.bfloat16), 'seq', scatter_d...  28.2 us
    reduce_scatter x1, waiting for transfers between devices, body(): lax.psum_scatter(partials[1][None].astype(jnp.bfloat16), 'seq', scatter_d...  27.9 us
    all_to_all x1, waiting for transfers between devices, body(): lax.all_to_all(grad_rows.reshape(experts, capacity, width), 'expert', spl...  25 us
    all_to_all x1, waiting for transfers between devices, body(): lax.all_to_all(outputs.reshape(experts, capacity, width), 'expert', split...  22.3 us
    all_to_all x1, waiting for transfers between devices, body(): lax.all_to_all(token_send, 'expert', split_axis=0, concat_axis=0, tiled=T...  21.1 us
    dot_general x6, matrix products, contract(): lax.dot_general(left, right, (((left_dim,), (right_dim,)), ((), ())), pre...  14.5 us
  transfers between devices with their start and end apart: 16, of which 8 were waited for; matrix products, arithmetic and copies ran while one was open for 21% of the time, Pallas kernels for 0%

profile of v1, /device:TPU:0, one launch (start us, length us, event | category | flops | bytes accessed | tf_op | source)
XLA Modules:
  0.0 338.0 jit_solution(5260260139604690959)
XLA Ops:
  7.9 5.6 %collective-permute-start = (bf16[128,1024]{1,0:T(8,128)(2,1)}, bf16[128,1024]{1,0:T(8,128)(2,1)}, u32[]{:S(2)}, u32[]{:S(2)}) collective-permute-start(bf16[128,1024]{1,0:T(8,128)(2,1)} %param.11), channel_id=1, source_target_pairs={{0,2},{1,3},{4,6},{5,7},{8,10},{9,11},{12,14},{13,15},{16,18},{17,... | collective-permute-start | bytes 786440 | tf_op jit(solution)/shard_map/ppermute | solution.py:10
  22.3 3.7 %scatter_custom_fusion = bf16[512,1024]{1,0:T(8,128)(2,1)} fusion(s32[512]{0:T(512)S(1)} %bitcast.76, f32[512,1024]{1,0:T(8,128)S(1)} %mul.56, f32[512]{0:T(512)S(1)} %reshape.113, bf16[]{:T(256)} %constant.7.clone.1), kind=kCustom, calls=%fused_computation.21 | custom fusion | flops 1048576 | bytes 3147778 | tf_op jit(solution)/shard_map/scatter | solution.py:69
  25.9 5.0 %all-to-all-start = ((bf16[4,128,1024]{2,1,0:T(8,128)(2,1)}), bf16[4,128,1024]{2,1,0:T(8,128)(2,1)}, u32[]{:S(2)}, u32[]{:S(2)}) async-start(bf16[4,128,1024]{2,1,0:T(8,128)(2,1)} %bitcast.1), calls=%async_computation | async-start | bytes 2097152 | tf_op jit(solution)/shard_map/all_to_all | solution.py:94
  33.6 14.0 %convolution_convert_fusion.4 = bf16[1,128,1024]{2,0,1:T(2,128)(2,1)S(1)} fusion(bf16[1,383,1024]{2,1,0:T(8,128)(2,1)S(1)} %fusion.27, bf16[256,1,1024]{2,0,1:T(8,128)(2,1)S(1)} %bitcast.74), kind=kOutput, calls=%fused_computation.17 | convolution fusion | flops 67239936 | bytes 1570816 | tf_op jit(solution)/shard_map/conv_general_dilated | solution.py:14
  49.1 4.2 %scatter_custom_fusion.1 = bf16[512,1024]{1,0:T(8,128)(2,1)} fusion(s32[512]{0:T(512)S(1)} %bitcast.77, bf16[512,1024]{1,0:T(8,128)(2,1)} %reshape.142, bf16[]{:T(256)} %constant.7.clone.1), kind=kCustom, calls=%fused_computation.49 | custom fusion | bytes 1049088 | tf_op jit(solution)/shard_map/scatter | solution.py:69
  53.4 3.0 all-to-all-done
  56.3 3.5 %all-to-all-start.1 = ((bf16[4,128,1024]{2,1,0:T(8,128)(2,1)}), bf16[4,128,1024]{2,1,0:T(8,128)(2,1)S(1)}, u32[]{:S(2)}, u32[]{:S(2)}) async-start(bf16[4,128,1024]{2,1,0:T(8,128)(2,1)} %bitcast.6), calls=%async_computation.1 | async-start | bytes 2097152 | tf_op jit(solution)/shard_map/all_to_all | solution.py:93
  60.6 3.3 fusion.20
  63.9 21.1 %all-to-all-done.1 = bf16[4,128,1024]{2,1,0:T(8,128)(2,1)S(1)} async-done(((bf16[4,128,1024]{2,1,0:T(8,128)(2,1)}), bf16[4,128,1024]{2,1,0:T(8,128)(2,1)S(1)}, u32[]{:S(2)}, u32[]{:S(2)}) %all-to-all-start.1) | async-done | bytes 1048608 | tf_op jit(solution)/shard_map/all_to_all | solution.py:93
  86.0 2.9 fusion.14
  88.9 4.1 %multiply_convert_fusion.2 = (bf16[512,512]{1,0:T(8,128)(2,1)}, bf16[512,512]{1,0:T(8,128)(2,1)S(1)}, bf16[512,512]{1,0:T(8,128)(2,1)S(1)}) fusion(f32[512,512]{1,0:T(8,128)} %fusion.14, f32[512,512]{1,0:T(8,128)} %fusion.20, bf16[512,1024]{1,0:T(8,128)(2,1)} %bitcast.68, bf16[1,1024,512]{2,1,0:T(8,128)(2,1)} %all-gather.6.cloned.1.call-done), kind=kOutput, calls=%fused_computation.35 | convolution fusion | flops 540803072 | bytes 5767168 | tf_op jit(solution)/shard_map/dot_general | solution.py:33
  96.3 3.5 %all-to-all-start.2 = ((bf16[4,128,1024]{2,1,0:T(8,128)(2,1)}), bf16[4,128,1024]{2,1,0:T(8,128)(2,1)S(1)}, u32[]{:S(2)}, u32[]{:S(2)}) async-start(bf16[4,128,1024]{2,1,0:T(8,128)(2,1)} %bitcast.65), calls=%async_computation.2 | async-start | bytes 2097152 | tf_op jit(solution)/shard_map/all_to_all | solution.py:102
  100.0 25.0 %all-to-all-done.2 = bf16[4,128,1024]{2,1,0:T(8,128)(2,1)S(1)} async-done(((bf16[4,128,1024]{2,1,0:T(8,128)(2,1)}), bf16[4,128,1024]{2,1,0:T(8,128)(2,1)S(1)}, u32[]{:S(2)}, u32[]{:S(2)}) %all-to-all-start.2) | async-done | bytes 1048608 | tf_op jit(solution)/shard_map/all_to_all | solution.py:102
  132.9 15.1 %fusion.8 = f32[1,256,1024]{2,0,1:T(1,128)S(1)} fusion(bf16[1,383,1024]{2,1,0:T(8,128)(2,1)} %copy-done.4, bf16[128,1,1024]{2,0,1:T(8,128)(2,1)S(1)} %bitcast.72), kind=kOutput, calls=%fused_computation.18 | convolution fusion | flops 67108864 | bytes 2095104 | tf_op jit(solution)/shard_map/conv_general_dilated | solution.py:14
  148.2 5.3 %rev.7 = f32[256,1024]{1,0:T(8,128)} reverse(f32[256,1024]{1,0:T(8,128)S(1)} %bitcast.64), dimensions={0} | reverse | bytes 2097152 | tf_op jit(solution)/shard_map/rev | solution.py:136
  153.6 3.2 fusion.4
  162.5 3.1 convolution_convert_fusion.3
  165.6 3.5 %all-to-all-start.3 = ((bf16[4,128,1024]{2,1,0:T(8,128)(2,1)}), bf16[4,128,1024]{2,1,0:T(8,128)(2,1)S(1)}, u32[]{:S(2)}, u32[]{:S(2)}) async-start(bf16[4,128,1024]{2,1,0:T(8,128)(2,1)} %bitcast.71), calls=%async_computation.3 | async-start | bytes 2097152 | tf_op jit(solution)/shard_map/all_to_all | solution.py:109
  172.0 22.3 %all-to-all-done.3 = bf16[4,128,1024]{2,1,0:T(8,128)(2,1)S(1)} async-done(((bf16[4,128,1024]{2,1,0:T(8,128)(2,1)}), bf16[4,128,1024]{2,1,0:T(8,128)(2,1)S(1)}, u32[]{:S(2)}, u32[]{:S(2)}) %all-to-all-start.3) | async-done | bytes 1048608 | tf_op jit(solution)/shard_map/all_to_all | solution.py:109
  200.7 14.0 %fusion.5 = bf16[1,128,1024]{2,0,1:T(2,128)(2,1)S(1)} fusion(bf16[1,383,1024]{2,1,0:T(8,128)(2,1)S(1)} %fusion.26, bf16[256,1,1024]{2,0,1:T(8,128)(2,1)S(1)} %bitcast.73), kind=kOutput, calls=%fused_computation.16 | convolution fusion | flops 67239936 | bytes 1570816 | tf_op jit(solution)/shard_map/conv_general_dilated | solution.py:14
  215.4 3.1 reduce-scatter.8.cloned.1.call-done
  218.6 27.9 %reduce-scatter.6.cloned.1.call-done = bf16[1,256,512]{2,1,0:T(8,128)(2,1)} async-done(((bf16[1,1024,512]{2,1,0:T(8,128)(2,1)}), bf16[1,256,512]{2,1,0:T(8,128)(2,1)}) %reduce-scatter.6.cloned.1.call-update) | async-done | bytes 262160 | tf_op jit(solution)/shard_map/reduce_scatter | solution.py:125
  246.5 28.2 %reduce-scatter.4.cloned.1.call-done = bf16[1,256,512]{2,1,0:T(8,128)(2,1)} async-done(((bf16[1,1024,512]{2,1,0:T(8,128)(2,1)}), bf16[1,256,512]{2,1,0:T(8,128)(2,1)}) %reduce-scatter.4.cloned.1.call-update) | async-done | bytes 262160 | tf_op jit(solution)/shard_map/reduce_scatter | solution.py:122
  274.6 54.2 %all-reduce.5.cloned.1.call-done = f32[256,1024]{1,0:T(8,128)} async-done(((f32[256,1024]{1,0:T(8,128)}), f32[256,1024]{1,0:T(8,128)}) %all-reduce.5.cloned.1.call-update) | async-done | bytes 1048592 | tf_op jit(solution)/shard_map/psum | solution.py:137
  (80 shorter events, 44.9 us)
Async XLA Ops:
  7.2 53.4 %all-gather.4.cloned.1.call-start = ((), (), s32[]{:S(2)}) async-start(), calls=%async_computation.7 | async-start | bytes 1310720 | tf_op jit(solution)/shard_map/all_gather | solution.py:84
  7.9 24.4 %collective-permute-start = (bf16[128,1024]{1,0:T(8,128)(2,1)}, bf16[128,1024]{1,0:T(8,128)(2,1)}, u32[]{:S(2)}, u32[]{:S(2)}) collective-permute-start(bf16[128,1024]{1,0:T(8,128)(2,1)} %param.11), channel_id=1, source_target_pairs={{0,2},{1,3},{4,6},{5,7},{8,10},{9,11},{12,14},{13,15},{16,18},{17,... | collective-permute-start | bytes 786440 | tf_op jit(solution)/shard_map/ppermute | solution.py:10
  13.5 18.9 %collective-permute-start.1 = (bf16[128,1024]{1,0:T(8,128)(2,1)}, bf16[128,1024]{1,0:T(8,128)(2,1)}, u32[]{:S(2)}, u32[]{:S(2)}) collective-permute-start(bf16[128,1024]{1,0:T(8,128)(2,1)} %param.11), channel_id=1, source_target_pairs={{0,1},{1,2},{2,3},{4,5},{5,6},{6,7},{8,9},{9,10},{10,11},{12,13},{... | collective-permute-start | bytes 786440 | tf_op jit(solution)/shard_map/ppermute | solution.py:10
  22.2 9.4 %copy-start.7 = (bf16[256,1024]{1,0:T(8,128)(2,1)S(1)}, bf16[256,1024]{1,0:T(8,128)(2,1)}, u32[]{:S(2)}) copy-start(bf16[256,1024]{1,0:T(8,128)(2,1)} %param.16) | copy-start | bytes 1572868
  25.9 6.5 %copy-start.9 = (bf16[128,1024]{1,0:T(8,128)(2,1)S(1)}, bf16[128,1024]{1,0:T(8,128)(2,1)}, u32[]{:S(2)}) copy-start(bf16[128,1024]{1,0:T(8,128)(2,1)} %param.11) | copy-start | bytes 786436
  25.9 30.4 %all-to-all-start = ((bf16[4,128,1024]{2,1,0:T(8,128)(2,1)}), bf16[4,128,1024]{2,1,0:T(8,128)(2,1)}, u32[]{:S(2)}, u32[]{:S(2)}) async-start(bf16[4,128,1024]{2,1,0:T(8,128)(2,1)} %bitcast.1), calls=%async_computation | async-start | bytes 2097152 | tf_op jit(solution)/shard_map/all_to_all | solution.py:94
  30.9 33.0 %all-gather.8.cloned.1.call-start = ((), (), s32[]{:S(2)}) async-start(), calls=%async_computation.9 | async-start | bytes 1310720 | tf_op jit(solution)/shard_map/all_gather | solution.py:82
  33.6 14.0 %copy-start.4 = (bf16[1,383,1024]{2,1,0:T(8,128)(2,1)}, bf16[1,383,1024]{2,1,0:T(8,128)(2,1)S(1)}, u32[]{:S(2)}) copy-start(bf16[1,383,1024]{2,1,0:T(8,128)(2,1)S(1)} %fusion.27) | copy-start | bytes 2353156
  56.3 28.7 %all-to-all-start.1 = ((bf16[4,128,1024]{2,1,0:T(8,128)(2,1)}), bf16[4,128,1024]{2,1,0:T(8,128)(2,1)S(1)}, u32[]{:S(2)}, u32[]{:S(2)}) async-start(bf16[4,128,1024]{2,1,0:T(8,128)(2,1)} %bitcast.6), calls=%async_computation.1 | async-start | bytes 2097152 | tf_op jit(solution)/shard_map/all_to_all | solution.py:93
  59.8 29.1 %all-gather.6.cloned.1.call-start = ((), (), s32[]{:S(2)}) async-start(), calls=%async_computation.8 | async-start | bytes 1310720 | tf_op jit(solution)/shard_map/all_gather | solution.py:83
  88.9 4.1 %copy-start = (bf16[1,1024,512]{2,1,0:T(8,128)(2,1)S(1)}, bf16[1,1024,512]{2,1,0:T(8,128)(2,1)}, u32[]{:S(2)}) copy-start(bf16[1,1024,512]{2,1,0:T(8,128)(2,1)} %all-gather.8.cloned.1.call-done) | copy-start | bytes 3145732
  93.0 3.3 copy-start.6
  93.0 1.6 copy-start.3
  96.3 28.7 %all-to-all-start.2 = ((bf16[4,128,1024]{2,1,0:T(8,128)(2,1)}), bf16[4,128,1024]{2,1,0:T(8,128)(2,1)S(1)}, u32[]{:S(2)}, u32[]{:S(2)}) async-start(bf16[4,128,1024]{2,1,0:T(8,128)(2,1)} %bitcast.65), calls=%async_computation.2 | async-start | bytes 2097152 | tf_op jit(solution)/shard_map/all_to_all | solution.py:102
  99.8 100.8 %all-reduce.3.cloned.1.call-start = ((), (), s32[]{:S(2)}) async-start(), calls=%async_computation.10 | async-start | bytes 2097152 | tf_op jit(solution)/shard_map/psum | solution.py:137
  153.5 3.3 copy-start.2
  153.6 65.0 %reduce-scatter.8.cloned.1.call-start = ((), (), s32[]{:S(2)}) async-start(), calls=%async_computation.14 | async-start | bytes 1310720 | tf_op jit(solution)/shard_map/reduce_scatter | solution.py:128
  156.8 89.7 %reduce-scatter.6.cloned.1.call-start = ((), (), s32[]{:S(2)}) async-start(), calls=%async_computation.13 | async-start | bytes 1310720 | tf_op jit(solution)/shard_map/reduce_scatter | solution.py:125
  159.7 115.0 %reduce-scatter.4.cloned.1.call-start = ((), (), s32[]{:S(2)}) async-start(), calls=%async_computation.12 | async-start | bytes 1310720 | tf_op jit(solution)/shard_map/reduce_scatter | solution.py:122
  165.6 28.7 %all-to-all-start.3 = ((bf16[4,128,1024]{2,1,0:T(8,128)(2,1)}), bf16[4,128,1024]{2,1,0:T(8,128)(2,1)S(1)}, u32[]{:S(2)}, u32[]{:S(2)}) async-start(bf16[4,128,1024]{2,1,0:T(8,128)(2,1)} %bitcast.71), calls=%async_computation.3 | async-start | bytes 2097152 | tf_op jit(solution)/shard_map/all_to_all | solution.py:109
  169.1 159.7 %all-reduce.5.cloned.1.call-start = ((), (), s32[]{:S(2)}) async-start(), calls=%async_computation.11 | async-start | bytes 2097152 | tf_op jit(solution)/shard_map/psum | solution.py:137
  169.2 30.3 %collective-permute-start.3 = (bf16[128,1024]{1,0:T(8,128)(2,1)S(1)}, bf16[128,1024]{1,0:T(8,128)(2,1)}, u32[]{:S(2)}, u32[]{:S(2)}) collective-permute-start(bf16[128,1024]{1,0:T(8,128)(2,1)S(1)} %reduce_sum.21), channel_id=1, source_target_pairs={{2,0},{3,1},{6,4},{7,5},{10,8},{11,9},{14,12},{15,13},{18,16},{19,... | collective-permute-start | bytes 786440 | tf_op jit(solution)/shard_map/ppermute | solution.py:10
  170.5 29.0 %collective-permute-start.2 = (bf16[128,1024]{1,0:T(8,128)(2,1)S(1)}, bf16[128,1024]{1,0:T(8,128)(2,1)}, u32[]{:S(2)}, u32[]{:S(2)}) collective-permute-start(bf16[128,1024]{1,0:T(8,128)(2,1)S(1)} %reduce_sum.21), channel_id=1, source_target_pairs={{1,0},{2,1},{3,2},{5,4},{6,5},{7,6},{9,8},{10,9},{11,10},{13,12},{... | collective-permute-start | bytes 786440 | tf_op jit(solution)/shard_map/ppermute | solution.py:10
  198.7 1.9 copy-start.8
  (2 other events, 1.8 us)
Sparse Core Ops, SparseCore 0:
  9.6 19.4 all-gather.3
  33.3 17.2 all-gather.7
  62.2 17.1 all-gather.5
  153.7 36.1 all-reduce.2
  193.0 25.5 reduce-scatter.7
  221.5 24.9 reduce-scatter.5
  249.7 24.8 reduce-scatter.3
  277.0 51.8 all-reduce.4
